TPU v7x, 128 devices: a whole 4x4x4 slice. The times are simulated.
128 devices in a mesh: gz: 8 (over x, core), xy: 16 (over y, z).
Axes of the slice: x: 4, y: 4, z: 4, core: 2. Of those that a mesh axis runs over, the one named last changes fastest.
Arguments:
- parent_feat: bfloat16 [128, 64, 2048], P(('gz', 'xy')), may hold values from -6 to 6
- parent_cell: int32 [128, 2048], P(('gz', 'xy')), may hold values from 0 to 255
- send_count: int32 [128, 128], P(('gz', 'xy')), may hold values from 1 to 16, as said below
- up_weight: bfloat16 [8, 64, 64], replicated, may hold values from -0.75 to 0.75
- conv_one: bfloat16 [27, 64, 64], replicated, may hold values from -0.15625 to 0.15625
- conv_two: bfloat16 [27, 64, 64], replicated, may hold values from -0.15625 to 0.15625
- child_mask: int32 [32, 8, 1024], P('xy', None, 'gz'), may hold values 0 or 1
- cotangent: bfloat16 [64, 32, 8, 1024], P(None, 'xy', None, 'gz'), may hold values from -6 to 6
Outputs:
- decoded: bfloat16 [64, 32, 8, 1024], P(None, 'xy', None, 'gz')
- grad_parent: bfloat16 [128, 64, 2048], P(('gz', 'xy'))
- grad_one: float32 [27, 64, 64], replicated
- grad_two: float32 [27, 64, 64], replicated
- grad_up: float32 [8, 64, 64], replicated
Inputs may be any that keep to these rules, and one draw needn't show every extreme that they name: `send_count`: some receiver gets 16 live slots from every sender, and every sender fills all 16 slots to some receiver. `parent_cell`: several slots may name the same parent voxel; their features add.
All inputs are finite; a program needn't handle non-finite values. No bound on the sum of `child_mask` on one device may be relied on, other than what follows from the above.
Results may differ from a plain program's by a relative error of at most 0.008.
Values may be sent and summed in bfloat16 or wider, within the bound.
No kernel may reach another device: no remote copies, remote signals or barrier semaphores. Data moves between devices by JAX's collectives and lax.ppermute only.
A program may use at most 64 MiB of HBM per device.

v0:
```python
import math
import jax
import jax.numpy as jnp
from jax import lax
from jax.sharding import PartitionSpec as P

OFFSETS = [(a, b, c) for a in (-1, 0, 1) for b in (-1, 0, 1) for c in (-1, 0, 1)]


def with_halo(shard, sides, width):
    for axis, dim in sides:
        devices, length = (lax.axis_size(axis), shard.shape[dim])
        up = [(i, (i + 1) % devices) for i in range(devices - 1)]
        down = [(j, i) for i, j in up]
        last = lax.slice_in_dim(shard, length - width, length, axis=dim)
        first = lax.slice_in_dim(shard, 0, width, axis=dim)
        before = lax.ppermute(last, axis, up)
        after = lax.ppermute(first, axis, down)
        shard = jnp.concatenate([before, shard, after], axis=dim)
    return shard


def extend(field):
    bordered = with_halo(field, (("xy", 1), ("gz", 3)), 1)
    return jnp.pad(bordered, ((0, 0), (0, 0), (1, 1), (0, 0)))


def window(padded, offset, direction, shape):
    nx, ny, nz = (shape[1], shape[2], shape[3])
    ox, oy, oz = (offset[0] * direction, offset[1] * direction, offset[2] * direction)
    part = padded[:, 1 + ox : 1 + ox + nx, 1 + oy : 1 + oy + ny, 1 + oz : 1 + oz + nz]
    return part.reshape(shape[0], -1)


def orient(matrix, direction):
    return matrix if direction > 0 else matrix.T


def convolve(padded, weights, direction, shape):
    total = jnp.zeros((shape[0], shape[1] * shape[2] * shape[3]), jnp.float32)
    for index, offset in enumerate(OFFSETS):
        total = total + jnp.dot(
            orient(weights[index], direction),
            window(padded, offset, direction, shape),
            preferred_element_type=jnp.float32,
        )
    return total.reshape(shape)


def weight_terms(delta, padded, shape):
    flat = delta.reshape(shape[0], -1)
    terms = [
        lax.dot_general(
            flat,
            window(padded, offset, 1, shape),
            (((1,), (1,)), ((), ())),
            preferred_element_type=jnp.float32,
        )
        for offset in OFFSETS
    ]
    return jnp.stack(terms)


def silu_slope(value):
    sig = jax.nn.sigmoid(value)
    return sig * (1.0 + value * (1.0 - sig))


def local(
    parent_feat, parent_cell, send_count, up_weight, conv_one, conv_two, child_mask, cotangent
):
    channels, size_x, size_y, size_z = cotangent.shape
    shape = cotangent.shape
    count_gz = lax.axis_size("gz")
    count_xy = lax.axis_size("xy")
    devices_all = count_gz * count_xy
    slot_total = parent_feat.shape[2]
    capacity = slot_total // devices_all
    half_x, half_y, half_z = (size_x // 2, size_y // 2, size_z // 2)
    parent_total = half_x * half_y * half_z
    slot_pos = jnp.arange(slot_total, dtype=jnp.int32) % capacity
    live = slot_pos < jnp.repeat(send_count[0], capacity)
    feats = jnp.where(live[None, :], parent_feat[0], jnp.zeros_like(parent_feat[0]))
    got_feat, got_cell = (
        lax.all_to_all(feats, ("gz", "xy"), split_axis=1, concat_axis=1, tiled=True),
        lax.all_to_all(parent_cell, ("gz", "xy"), split_axis=1, concat_axis=1, tiled=True),
    )
    got_cell = got_cell.reshape(slot_total)
    onehot = (got_cell[:, None] == jnp.arange(parent_total, dtype=jnp.int32)[None, :]).astype(
        jnp.bfloat16
    )
    parent_grid = jnp.dot(got_feat, onehot, preferred_element_type=jnp.float32).astype(jnp.bfloat16)
    up8 = jnp.einsum("ocd,dq->ocq", up_weight, parent_grid, preferred_element_type=jnp.float32)
    up = (
        up8.reshape(2, 2, 2, channels, half_x, half_y, half_z)
        .transpose(3, 4, 0, 5, 1, 6, 2)
        .reshape(shape)
    )
    maskf = child_mask.astype(jnp.float32)
    lifted = (maskf * up).astype(jnp.bfloat16)
    lifted_pad = extend(lifted)
    first_pre = convolve(lifted_pad, conv_one, 1, shape)
    first_act = (maskf * jax.nn.silu(first_pre)).astype(jnp.bfloat16)
    first_pad = extend(first_act)
    second_pre = convolve(first_pad, conv_two, 1, shape)
    decoded = (maskf * jax.nn.silu(second_pre)).astype(jnp.bfloat16)
    delta_two = (cotangent.astype(jnp.float32) * maskf * silu_slope(second_pre)).astype(
        jnp.bfloat16
    )
    term_two = weight_terms(delta_two, first_pad, shape)
    back_one = convolve(extend(delta_two), conv_two, -1, shape)
    delta_one = (back_one * maskf * silu_slope(first_pre)).astype(jnp.bfloat16)
    term_one = weight_terms(delta_one, lifted_pad, shape)
    delta_up = (convolve(extend(delta_one), conv_one, -1, shape) * maskf).astype(jnp.bfloat16)
    du8 = (
        delta_up.reshape(channels, half_x, 2, half_y, 2, half_z, 2)
        .transpose(2, 4, 6, 0, 1, 3, 5)
        .reshape(8, channels, parent_total)
    )
    term_up = jnp.einsum("ocq,dq->ocd", du8, parent_grid, preferred_element_type=jnp.float32)
    delta_parent = jnp.einsum(
        "ocd,ocq->dq", up_weight, du8, preferred_element_type=jnp.float32
    ).astype(jnp.bfloat16)
    slot_grad = lax.dot_general(
        delta_parent, onehot, (((1,), (1,)), ((), ())), preferred_element_type=jnp.float32
    ).astype(jnp.bfloat16)
    returned = lax.all_to_all(slot_grad, ("gz", "xy"), split_axis=1, concat_axis=1, tiled=True)
    grad_parent = jnp.where(live[None, :], returned, jnp.zeros_like(returned))[None]
    sum_one, sum_two, sum_up = lax.psum((term_one, term_two, term_up), ("gz", "xy"))
    scale = 1.0 / math.sqrt(size_x * count_xy * size_y * size_z * count_gz)
    return (decoded, grad_parent, sum_one * scale, sum_two * scale, sum_up * scale)


def solution(mesh):
    placed = (
        P(("gz", "xy"), None, None),
        P(("gz", "xy"), None),
        P(("gz", "xy"), None),
        P(),
        P(),
        P(),
        P("xy", None, "gz"),
        P(None, "xy", None, "gz"),
    )
    return jax.shard_map(
        local,
        mesh=mesh,
        in_specs=placed,
        out_specs=(P(None, "xy", None, "gz"), P(("gz", "xy"), None, None), P(), P(), P()),
        check_vma=False,
    )
```

profile of v0, /device:TPU:1, one launch (start us, length us, event | category | flops | bytes accessed | tf_op | source)
XLA Modules:
  0.0 432.3 jit_solution(10108309760339999828)
XLA Ops:
  9.8 11.5 %all-to-all-start.1 = ((s32[1,128,16]{2,0,1:T(1,128)}), s32[1,128,16]{2,0,1:T(1,128)S(1)}, u32[]{:S(2)}, u32[]{:S(2)}) async-start(s32[1,128,16]{2,0,1:T(1,128)} %bitcast.3), calls=%async_computation.1 | async-start | bytes 131072 | tf_op jit(solution)/shard_map/all_to_all | solution.py:86
  24.6 6.2 %all-to-all-done.1 = s32[1,128,16]{2,0,1:T(1,128)S(1)} async-done(((s32[1,128,16]{2,0,1:T(1,128)}), s32[1,128,16]{2,0,1:T(1,128)S(1)}, u32[]{:S(2)}, u32[]{:S(2)}) %all-to-all-start.1) | async-done | bytes 8224 | tf_op jit(solution)/shard_map/all_to_all | solution.py:86
  30.8 4.5 %all-to-all-start = ((bf16[128,2,512]{2,1,0:T(2,128)(2,1)}), bf16[128,2,512]{2,1,0:T(2,128)(2,1)S(1)}, u32[]{:S(2)}, u32[]{:S(2)}) async-start(bf16[128,2,512]{2,1,0:T(2,128)(2,1)} %reshape.685), calls=%async_computation | async-start | bytes 524288 | tf_op jit(solution)/shard_map/all_to_all | solution.py:85
  36.8 9.8 %all-to-all-done = bf16[128,2,512]{2,1,0:T(2,128)(2,1)S(1)} async-done(((bf16[128,2,512]{2,1,0:T(2,128)(2,1)}), bf16[128,2,512]{2,1,0:T(2,128)(2,1)S(1)}, u32[]{:S(2)}, u32[]{:S(2)}) %all-to-all-start) | async-done | bytes 262176 | tf_op jit(solution)/shard_map/all_to_all | solution.py:85
  53.9 3.6 collective-permute-done.1
  57.8 4.3 collective-permute-start.2
  68.2 4.4 %collective-permute-done.3 = bf16[64,4,8,1]{3,0,2,1:T(8,128)(2,1)S(1)} collective-permute-done((bf16[64,4,8,1]{3,0,2,1:T(8,128)(2,1)S(1)}, bf16[64,4,8,1]{3,0,2,1:T(8,128)(2,1)S(1)}, u32[]{:S(2)}, u32[]{:S(2)}) %collective-permute-start.3) | collective-permute-done | bytes 4128 | tf_op jit(solution)/shard_map/ppermute | solution.py:18
  96.8 3.8 collective-permute-done.5
  102.5 4.1 collective-permute-start.6
  113.1 4.4 %collective-permute-done.7 = bf16[64,4,8,1]{3,0,2,1:T(8,128)(2,1)} collective-permute-done((bf16[64,4,8,1]{3,0,2,1:T(8,128)(2,1)}, bf16[64,4,8,1]{3,0,2,1:T(8,128)(2,1)}, u32[]{:S(2)}, u32[]{:S(2)}) %collective-permute-start.7) | collective-permute-done | bytes 4128 | tf_op jit(solution)/shard_map/ppermute | solution.py:18
  149.3 5.2 %collective-permute-start.8 = (bf16[64,1,8,128]{3,0,2,1:T(8,128)(2,1)S(1)}, bf16[64,1,8,128]{3,0,2,1:T(8,128)(2,1)S(1)}, u32[]{:S(2)}, u32[]{:S(2)}) collective-permute-start(bf16[64,1,8,128]{3,0,2,1:T(8,128)(2,1)S(1)} %get-tuple-element.144), channel_id=1, source_target_pairs={{0,1},{1,2},{2,3},{3,4},{4,5},{5,6},{6,7},{7,8},{8,9},{9,10},{10,1... | collective-permute-start | bytes 393224 | tf_op jit(solution)/shard_map/ppermute | solution.py:17
  156.4 3.8 collective-permute-done.9
  160.6 3.8 collective-permute-start.10
  166.8 3.7 collective-permute-done.10
  170.5 4.4 %collective-permute-done.11 = bf16[64,4,8,1]{3,0,2,1:T(8,128)(2,1)S(1)} collective-permute-done((bf16[64,4,8,1]{3,0,2,1:T(8,128)(2,1)S(1)}, bf16[64,4,8,1]{3,0,2,1:T(8,128)(2,1)S(1)}, u32[]{:S(2)}, u32[]{:S(2)}) %collective-permute-start.11) | collective-permute-done | bytes 4128 | tf_op jit(solution)/shard_map/ppermute | solution.py:18
  203.5 3.5 collective-permute-start.12
  208.9 3.8 collective-permute-done.13
  213.0 4.1 collective-permute-start.14
  219.4 3.9 collective-permute-done.14
  223.3 4.4 %collective-permute-done.15 = bf16[64,4,8,1]{3,0,2,1:T(8,128)(2,1)S(1)} collective-permute-done((bf16[64,4,8,1]{3,0,2,1:T(8,128)(2,1)S(1)}, bf16[64,4,8,1]{3,0,2,1:T(8,128)(2,1)S(1)}, u32[]{:S(2)}, u32[]{:S(2)}) %collective-permute-start.15) | collective-permute-done | bytes 4128 | tf_op jit(solution)/shard_map/ppermute | solution.py:18
  253.7 7.1 %all-to-all-start.2 = ((bf16[128,2,512]{2,1,0:T(2,128)(2,1)}), bf16[128,2,512]{2,1,0:T(2,128)(2,1)S(1)}, u32[]{:S(2)}, u32[]{:S(2)}) async-start(bf16[128,2,512]{2,1,0:T(2,128)(2,1)} %reshape.687), calls=%async_computation.2 | async-start | bytes 524288 | tf_op jit(solution)/shard_map/all_to_all | solution.py:127
  262.7 9.3 %all-to-all-done.2 = bf16[128,2,512]{2,1,0:T(2,128)(2,1)S(1)} async-done(((bf16[128,2,512]{2,1,0:T(2,128)(2,1)}), bf16[128,2,512]{2,1,0:T(2,128)(2,1)S(1)}, u32[]{:S(2)}, u32[]{:S(2)}) %all-to-all-start.2) | async-done | bytes 262176 | tf_op jit(solution)/shard_map/all_to_all | solution.py:127
  273.6 147.1 %all-reduce.7.cloned.1.call-done = (f32[27,64,64]{2,1,0:T(8,128)}, f32[27,64,64]{2,1,0:T(8,128)}, f32[8,64,64]{2,1,0:T(8,128)}) async-done(((f32[27,64,64]{2,1,0:T(8,128)}, f32[27,64,64]{2,1,0:T(8,128)}, f32[8,64,64]{2,1,0:T(8,128)}), (f32[27,64,64]{2,1,0:T(8,128)}, f32[27,64,64]{2,1,0:T(8,128)}, f32[8,64,64]{2,1,0:T(8,128)})) %all-reduce.7.cloned.1.call-update) | async-done | bytes 1015824 | tf_op jit(solution)/shard_map/psum | solution.py:129
  422.4 2.9 broadcast_multiply_fusion
  (429 shorter events, 152.2 us)
Async XLA Ops:
  7.2 40.4 %copy-start = (bf16[8,64,64]{2,1,0:T(8,128)(2,1)S(1)}, bf16[8,64,64]{2,1,0:T(8,128)(2,1)}, u32[]{:S(2)}) copy-start(bf16[8,64,64]{2,1,0:T(8,128)(2,1)} %param.11) | copy-start | bytes 196612
  9.8 21.0 %all-to-all-start.1 = ((s32[1,128,16]{2,0,1:T(1,128)}), s32[1,128,16]{2,0,1:T(1,128)S(1)}, u32[]{:S(2)}, u32[]{:S(2)}) async-start(s32[1,128,16]{2,0,1:T(1,128)} %bitcast.3), calls=%async_computation.1 | async-start | bytes 131072 | tf_op jit(solution)/shard_map/all_to_all | solution.py:86
  23.2 12.0 %copy-start.33 = (s32[2,8,128]{2,1,0:T(8,128)S(1)}, s32[2,8,128]{2,1,0:T(8,128)}, u32[]{:S(2)}) copy-start(s32[2,8,128]{2,1,0:T(8,128)} %param.14) | copy-start | bytes 24580
  30.8 15.7 %all-to-all-start = ((bf16[128,2,512]{2,1,0:T(2,128)(2,1)}), bf16[128,2,512]{2,1,0:T(2,128)(2,1)S(1)}, u32[]{:S(2)}, u32[]{:S(2)}) async-start(bf16[128,2,512]{2,1,0:T(2,128)(2,1)} %reshape.685), calls=%async_computation | async-start | bytes 524288 | tf_op jit(solution)/shard_map/all_to_all | solution.py:85
  49.3 4.6 %collective-permute-start = (bf16[64,1,8,128]{3,0,2,1:T(8,128)(2,1)S(1)}, bf16[64,1,8,128]{3,0,2,1:T(8,128)(2,1)S(1)}, u32[]{:S(2)}, u32[]{:S(2)}) collective-permute-start(bf16[64,1,8,128]{3,0,2,1:T(8,128)(2,1)S(1)} %get-tuple-element.148), channel_id=1, source_target_pairs={{0,1},{1,2},{2,3},{3,4},{4,5},{5,6},{6,7},{7,8},{8,9},{9,10},{10,1... | collective-permute-start | bytes 393224 | tf_op jit(solution)/shard_map/ppermute | solution.py:17
  51.8 5.7 %collective-permute-start.1 = (bf16[64,1,8,128]{3,0,2,1:T(8,128)(2,1)S(1)}, bf16[64,1,8,128]{3,0,2,1:T(8,128)(2,1)S(1)}, u32[]{:S(2)}, u32[]{:S(2)}) collective-permute-start(bf16[64,1,8,128]{3,0,2,1:T(8,128)(2,1)S(1)} %get-tuple-element.149), channel_id=1, source_target_pairs={{1,0},{2,1},{3,2},{4,3},{5,4},{6,5},{7,6},{8,7},{9,8},{10,9},{11,1... | collective-permute-start | bytes 393224 | tf_op jit(solution)/shard_map/ppermute | solution.py:18
  53.9 18.7 %copy-start.17 = (bf16[64,1,8,128]{3,0,2,1:T(8,128)(2,1)}, bf16[64,1,8,128]{3,0,2,1:T(8,128)(2,1)S(1)}, u32[]{:S(2)}) copy-start(bf16[64,1,8,128]{3,0,2,1:T(8,128)(2,1)S(1)} %collective-permute-done) | copy-start | bytes 393220
  57.8 10.4 %collective-permute-start.2 = (bf16[64,4,8,1]{3,0,2,1:T(8,128)(2,1)S(1)}, bf16[64,4,8,1]{3,0,2,1:T(8,128)(2,1)S(1)}, u32[]{:S(2)}, u32[]{:S(2)}) collective-permute-start(bf16[64,4,8,1]{3,0,2,1:T(8,128)(2,1)S(1)} %get-tuple-element.132), channel_id=1, source_target_pairs={{0,16},{16,32},{32,48},{48,64},{64,80},{80,96},{96,112},{1,17},{17... | collective-permute-start | bytes 12296 | tf_op jit(solution)/shard_map/ppermute | solution.py:17
  62.1 10.5 %collective-permute-start.3 = (bf16[64,4,8,1]{3,0,2,1:T(8,128)(2,1)S(1)}, bf16[64,4,8,1]{3,0,2,1:T(8,128)(2,1)S(1)}, u32[]{:S(2)}, u32[]{:S(2)}) collective-permute-start(bf16[64,4,8,1]{3,0,2,1:T(8,128)(2,1)S(1)} %get-tuple-element.133), channel_id=1, source_target_pairs={{16,0},{32,16},{48,32},{64,48},{80,64},{96,80},{112,96},{17,1},{33... | collective-permute-start | bytes 12296 | tf_op jit(solution)/shard_map/ppermute | solution.py:18
  77.2 10.8 %copy-start.5 = (bf16[64,2,8,128]{3,0,2,1:T(8,128)(2,1)}, bf16[64,2,8,128]{3,0,2,1:T(8,128)(2,1)S(1)}, u32[]{:S(2)}) copy-start(bf16[64,2,8,128]{3,0,2,1:T(8,128)(2,1)S(1)} %get-tuple-element.141) | copy-start | bytes 786436
  92.9 3.9 collective-permute-start.4
  94.9 5.7 %collective-permute-start.5 = (bf16[64,1,8,128]{3,0,2,1:T(8,128)(2,1)S(1)}, bf16[64,1,8,128]{3,0,2,1:T(8,128)(2,1)S(1)}, u32[]{:S(2)}, u32[]{:S(2)}) collective-permute-start(bf16[64,1,8,128]{3,0,2,1:T(8,128)(2,1)S(1)} %get-tuple-element.147), channel_id=1, source_target_pairs={{1,0},{2,1},{3,2},{4,3},{5,4},{6,5},{7,6},{8,7},{9,8},{10,9},{11,1... | collective-permute-start | bytes 393224 | tf_op jit(solution)/shard_map/ppermute | solution.py:18
  102.5 10.6 %collective-permute-start.6 = (bf16[64,4,8,1]{3,0,2,1:T(8,128)(2,1)}, bf16[64,4,8,1]{3,0,2,1:T(8,128)(2,1)}, u32[]{:S(2)}, u32[]{:S(2)}) collective-permute-start(bf16[64,4,8,1]{3,0,2,1:T(8,128)(2,1)} %get-tuple-element.130), channel_id=1, source_target_pairs={{0,16},{16,32},{32,48},{48,64},{64,80},{80,96},{96,112},{1,17},{17... | collective-permute-start | bytes 12296 | tf_op jit(solution)/shard_map/ppermute | solution.py:17
  106.7 10.8 %collective-permute-start.7 = (bf16[64,4,8,1]{3,0,2,1:T(8,128)(2,1)}, bf16[64,4,8,1]{3,0,2,1:T(8,128)(2,1)}, u32[]{:S(2)}, u32[]{:S(2)}) collective-permute-start(bf16[64,4,8,1]{3,0,2,1:T(8,128)(2,1)} %get-tuple-element.131), channel_id=1, source_target_pairs={{16,0},{32,16},{48,32},{64,48},{80,64},{96,80},{112,96},{17,1},{33... | collective-permute-start | bytes 12296 | tf_op jit(solution)/shard_map/ppermute | solution.py:18
  149.3 7.2 %collective-permute-start.8 = (bf16[64,1,8,128]{3,0,2,1:T(8,128)(2,1)S(1)}, bf16[64,1,8,128]{3,0,2,1:T(8,128)(2,1)S(1)}, u32[]{:S(2)}, u32[]{:S(2)}) collective-permute-start(bf16[64,1,8,128]{3,0,2,1:T(8,128)(2,1)S(1)} %get-tuple-element.144), channel_id=1, source_target_pairs={{0,1},{1,2},{2,3},{3,4},{4,5},{5,6},{6,7},{7,8},{8,9},{9,10},{10,1... | collective-permute-start | bytes 393224 | tf_op jit(solution)/shard_map/ppermute | solution.py:17
  154.5 5.7 %collective-permute-start.9 = (bf16[64,1,8,128]{3,0,2,1:T(8,128)(2,1)S(1)}, bf16[64,1,8,128]{3,0,2,1:T(8,128)(2,1)S(1)}, u32[]{:S(2)}, u32[]{:S(2)}) collective-permute-start(bf16[64,1,8,128]{3,0,2,1:T(8,128)(2,1)S(1)} %get-tuple-element.145), channel_id=1, source_target_pairs={{1,0},{2,1},{3,2},{4,3},{5,4},{6,5},{7,6},{8,7},{9,8},{10,9},{11,1... | collective-permute-start | bytes 393224 | tf_op jit(solution)/shard_map/ppermute | solution.py:18
  160.6 9.9 %collective-permute-start.10 = (bf16[64,4,8,1]{3,0,2,1:T(8,128)(2,1)S(1)}, bf16[64,4,8,1]{3,0,2,1:T(8,128)(2,1)S(1)}, u32[]{:S(2)}, u32[]{:S(2)}) collective-permute-start(bf16[64,4,8,1]{3,0,2,1:T(8,128)(2,1)S(1)} %get-tuple-element.128), channel_id=1, source_target_pairs={{0,16},{16,32},{32,48},{48,64},{64,80},{80,96},{96,112},{1,17},{17... | collective-permute-start | bytes 12296 | tf_op jit(solution)/shard_map/ppermute | solution.py:17
  164.4 10.5 %collective-permute-start.11 = (bf16[64,4,8,1]{3,0,2,1:T(8,128)(2,1)S(1)}, bf16[64,4,8,1]{3,0,2,1:T(8,128)(2,1)S(1)}, u32[]{:S(2)}, u32[]{:S(2)}) collective-permute-start(bf16[64,4,8,1]{3,0,2,1:T(8,128)(2,1)S(1)} %get-tuple-element.129), channel_id=1, source_target_pairs={{16,0},{32,16},{48,32},{64,48},{80,64},{96,80},{112,96},{17,1},{33... | collective-permute-start | bytes 12296 | tf_op jit(solution)/shard_map/ppermute | solution.py:18
  203.5 5.4 %collective-permute-start.12 = (bf16[64,1,8,128]{3,0,2,1:T(8,128)(2,1)S(1)}, bf16[64,1,8,128]{3,0,2,1:T(8,128)(2,1)S(1)}, u32[]{:S(2)}, u32[]{:S(2)}) collective-permute-start(bf16[64,1,8,128]{3,0,2,1:T(8,128)(2,1)S(1)} %get-tuple-element.142), channel_id=1, source_target_pairs={{0,1},{1,2},{2,3},{3,4},{4,5},{5,6},{6,7},{7,8},{8,9},{9,10},{10,1... | collective-permute-start | bytes 393224 | tf_op jit(solution)/shard_map/ppermute | solution.py:17
  207.0 5.7 %collective-permute-start.13 = (bf16[64,1,8,128]{3,0,2,1:T(8,128)(2,1)S(1)}, bf16[64,1,8,128]{3,0,2,1:T(8,128)(2,1)S(1)}, u32[]{:S(2)}, u32[]{:S(2)}) collective-permute-start(bf16[64,1,8,128]{3,0,2,1:T(8,128)(2,1)S(1)} %get-tuple-element.143), channel_id=1, source_target_pairs={{1,0},{2,1},{3,2},{4,3},{5,4},{6,5},{7,6},{8,7},{9,8},{10,9},{11,1... | collective-permute-start | bytes 393224 | tf_op jit(solution)/shard_map/ppermute | solution.py:18
  213.0 10.2 %collective-permute-start.14 = (bf16[64,4,8,1]{3,0,2,1:T(8,128)(2,1)S(1)}, bf16[64,4,8,1]{3,0,2,1:T(8,128)(2,1)S(1)}, u32[]{:S(2)}, u32[]{:S(2)}) collective-permute-start(bf16[64,4,8,1]{3,0,2,1:T(8,128)(2,1)S(1)} %get-tuple-element.126), channel_id=1, source_target_pairs={{0,16},{16,32},{32,48},{48,64},{64,80},{80,96},{96,112},{1,17},{17... | collective-permute-start | bytes 12296 | tf_op jit(solution)/shard_map/ppermute | solution.py:17
  217.2 10.5 %collective-permute-start.15 = (bf16[64,4,8,1]{3,0,2,1:T(8,128)(2,1)S(1)}, bf16[64,4,8,1]{3,0,2,1:T(8,128)(2,1)S(1)}, u32[]{:S(2)}, u32[]{:S(2)}) collective-permute-start(bf16[64,4,8,1]{3,0,2,1:T(8,128)(2,1)S(1)} %get-tuple-element.127), channel_id=1, source_target_pairs={{16,0},{32,16},{48,32},{64,48},{80,64},{96,80},{112,96},{17,1},{33... | collective-permute-start | bytes 12296 | tf_op jit(solution)/shard_map/ppermute | solution.py:18
  253.7 18.3 %all-to-all-start.2 = ((bf16[128,2,512]{2,1,0:T(2,128)(2,1)}), bf16[128,2,512]{2,1,0:T(2,128)(2,1)S(1)}, u32[]{:S(2)}, u32[]{:S(2)}) async-start(bf16[128,2,512]{2,1,0:T(2,128)(2,1)} %reshape.687), calls=%async_computation.2 | async-start | bytes 524288 | tf_op jit(solution)/shard_map/all_to_all | solution.py:127
  260.8 159.9 %all-reduce.7.cloned.1.call-start = ((), (), s32[]{:S(2)}) async-start(), calls=%async_computation.3 | async-start | bytes 4063232 | tf_op jit(solution)/shard_map/psum | solution.py:129
  (33 other events, 92.0 us)
Sparse Core Ops, SparseCore 0:
  267.6 153.0 all-reduce.6
where the time goes:
time: 441 us; the launch traced here: 432 us
  waiting for transfers between devices  219 us (50%)
  starting transfers between devices  66 us (15%)
  matrix products  65.7 us (15%)
  local copies, waits for them, and re-layouts  41.5 us (9%)
  other arithmetic  23.5 us (5%)
  between operations  16.7 us (4%)
    psum x1, waiting for transfers between devices, local(): lax.psum((term_one, term_two, term_up), ('gz', 'xy'))  147 us
    dot_general x108, matrix products, convolve(): jnp.dot(orient(weights[index], direction), window(padded, offset, directi...  50.1 us
    ppermute x8, waiting for transfers between devices, with_halo(): after = lax.ppermute(first, axis, down)  32.5 us
    ppermute x8, starting transfers between devices, with_halo(): before = lax.ppermute(last, axis, up)  29.5 us
    slice x108, local copies, waits for them, and re-layouts, window(): part = padded[:, 1 + ox:1 + ox + nx, 1 + oy:1 + oy + ny, 1 + oz:1 + oz + nz]  23.1 us
    ppermute x8, waiting for transfers between devices, with_halo(): before = lax.ppermute(last, axis, up)  13.9 us
    ppermute x8, starting transfers between devices, with_halo(): after = lax.ppermute(first, axis, down)  13.4 us
    dot_general x54, matrix products, weight_terms(): lax.dot_general(flat, window(padded, offset, 1, shape), (((1,), (1,)), ((...  13.2 us
  transfers between devices with their start and end apart: 20, of which 20 were waited for; matrix products, arithmetic and copies ran while one was open for 3% of the time, Pallas kernels for 0%

commit v1 on v0

--- a/solution.py
+++ b/solution.py
@@ -126,7 +126,7 @@
     ).astype(jnp.bfloat16)
     returned = lax.all_to_all(slot_grad, ("gz", "xy"), split_axis=1, concat_axis=1, tiled=True)
     grad_parent = jnp.where(live[None, :], returned, jnp.zeros_like(returned))[None]
-    sum_one, sum_two, sum_up = lax.psum((term_one, term_two, term_up), ("gz", "xy"))
+    sum_one, sum_two, sum_up = lax.psum(lax.psum((term_one, term_two, term_up), "xy"), "gz")
     scale = 1.0 / math.sqrt(size_x * count_xy * size_y * size_z * count_gz)
     return (decoded, grad_parent, sum_one * scale, sum_two * scale, sum_up * scale)
 

time: 441 us -> 423 us (0.959)
  the two profiles are of different devices: /device:TPU:1 before, /device:TPU:0 now
where the time goes in v1:
time: 423 us; the launch traced here: 415 us
  waiting for transfers between devices  197 us (47%)
  starting transfers between devices  80.4 us (19%)
  matrix products  65.8 us (16%)
  local copies, waits for them, and re-layouts  36.6 us (9%)
  other arithmetic  18.7 us (4%)
  between operations  16.4 us (4%)
    psum x1, waiting for transfers between devices, local(): lax.psum((term_one, term_two, term_up), 'xy')  83.2 us
    psum x1, waiting for transfers between devices, local(): lax.psum(lax.psum((term_one, term_two, term_up), 'xy'), 'gz')  65 us
    dot_general x108, matrix products, convolve(): jnp.dot(orient(weights[index], direction), window(padded, offset, directi...  50.2 us
    ppermute x8, starting transfers between devices, with_halo(): before = lax.ppermute(last, axis, up)  38.7 us
    ppermute x8, waiting for transfers between devices, with_halo(): after = lax.ppermute(first, axis, down)  29 us
    slice x108, local copies, waits for them, and re-layouts, window(): part = padded[:, 1 + ox:1 + ox + nx, 1 + oy:1 + oy + ny, 1 + oz:1 + oz + nz]  23.1 us
    all_to_all x1, starting transfers between devices, local(): lax.all_to_all(slot_grad, ('gz', 'xy'), split_axis=1, concat_axis=1, tile...  14.9 us
    dot_general x54, matrix products, weight_terms(): lax.dot_general(flat, window(padded, offset, 1, shape), (((1,), (1,)), ((...  13.2 us
  transfers between devices with their start and end apart: 21, of which 16 were waited for; matrix products, arithmetic and copies ran while one was open for 3% of the time, Pallas kernels for 0%

profile of v1, /device:TPU:0, one launch (start us, length us, event | category | flops | bytes accessed | tf_op | source)
XLA Modules:
  0.0 415.0 jit_solution(15277234358369274785)
XLA Ops:
  9.8 11.2 %all-to-all-start.1 = ((s32[1,128,16]{2,0,1:T(1,128)}), s32[1,128,16]{2,0,1:T(1,128)S(1)}, u32[]{:S(2)}, u32[]{:S(2)}) async-start(s32[1,128,16]{2,0,1:T(1,128)} %bitcast.3), calls=%async_computation.1 | async-start | bytes 131072 | tf_op jit(solution)/shard_map/all_to_all | solution.py:86
  24.3 6.1 %all-to-all-done.1 = s32[1,128,16]{2,0,1:T(1,128)S(1)} async-done(((s32[1,128,16]{2,0,1:T(1,128)}), s32[1,128,16]{2,0,1:T(1,128)S(1)}, u32[]{:S(2)}, u32[]{:S(2)}) %all-to-all-start.1) | async-done | bytes 8224 | tf_op jit(solution)/shard_map/all_to_all | solution.py:86
  30.4 4.6 %all-to-all-start = ((bf16[128,2,512]{2,1,0:T(2,128)(2,1)}), bf16[128,2,512]{2,1,0:T(2,128)(2,1)S(1)}, u32[]{:S(2)}, u32[]{:S(2)}) async-start(bf16[128,2,512]{2,1,0:T(2,128)(2,1)} %reshape.685), calls=%async_computation | async-start | bytes 524288 | tf_op jit(solution)/shard_map/all_to_all | solution.py:85
  36.0 9.9 %all-to-all-done = bf16[128,2,512]{2,1,0:T(2,128)(2,1)S(1)} async-done(((bf16[128,2,512]{2,1,0:T(2,128)(2,1)}), bf16[128,2,512]{2,1,0:T(2,128)(2,1)S(1)}, u32[]{:S(2)}, u32[]{:S(2)}) %all-to-all-start) | async-done | bytes 262176 | tf_op jit(solution)/shard_map/all_to_all | solution.py:85
  48.6 2.7 collective-permute-start
  54.1 4.2 %collective-permute-done.1 = bf16[64,1,8,128]{3,0,2,1:T(8,128)(2,1)S(1)} collective-permute-done((bf16[64,1,8,128]{3,0,2,1:T(8,128)(2,1)S(1)}, bf16[64,1,8,128]{3,0,2,1:T(8,128)(2,1)S(1)}, u32[]{:S(2)}, u32[]{:S(2)}) %collective-permute-start.1) | collective-permute-done | bytes 131104 | tf_op jit(solution)/shard_map/ppermute | solution.py:18
  61.2 1.7 fusion.118
  83.8 2.3 collective-permute-start.4
  88.5 4.4 %collective-permute-done.5 = bf16[64,1,8,128]{3,0,2,1:T(8,128)(2,1)S(1)} collective-permute-done((bf16[64,1,8,128]{3,0,2,1:T(8,128)(2,1)S(1)}, bf16[64,1,8,128]{3,0,2,1:T(8,128)(2,1)S(1)}, u32[]{:S(2)}, u32[]{:S(2)}) %collective-permute-start.5) | collective-permute-done | bytes 131104 | tf_op jit(solution)/shard_map/ppermute | solution.py:18
  93.2 7.7 %collective-permute-start.6 = (bf16[64,4,8,1]{3,0,2,1:T(8,128)(2,1)S(1)}, bf16[64,4,8,1]{3,0,2,1:T(8,128)(2,1)S(1)}, u32[]{:S(2)}, u32[]{:S(2)}) collective-permute-start(bf16[64,4,8,1]{3,0,2,1:T(8,128)(2,1)S(1)} %get-tuple-element.133), channel_id=1, source_target_pairs={{0,16},{16,32},{32,48},{48,64},{64,80},{80,96},{96,112},{1,17},{17... | collective-permute-start | bytes 12296 | tf_op jit(solution)/shard_map/ppermute | solution.py:17
  100.9 1.9 collective-permute-start.7
  102.8 3.6 collective-permute-done.7
  133.3 5.5 %collective-permute-start.8 = (bf16[64,1,8,128]{3,0,2,1:T(8,128)(2,1)S(1)}, bf16[64,1,8,128]{3,0,2,1:T(8,128)(2,1)S(1)}, u32[]{:S(2)}, u32[]{:S(2)}) collective-permute-start(bf16[64,1,8,128]{3,0,2,1:T(8,128)(2,1)S(1)} %get-tuple-element.147), channel_id=1, source_target_pairs={{0,1},{1,2},{2,3},{3,4},{4,5},{5,6},{6,7},{7,8},{8,9},{9,10},{10,1... | collective-permute-start | bytes 393224 | tf_op jit(solution)/shard_map/ppermute | solution.py:17
  141.3 4.4 %collective-permute-done.9 = bf16[64,1,8,128]{3,0,2,1:T(8,128)(2,1)S(1)} collective-permute-done((bf16[64,1,8,128]{3,0,2,1:T(8,128)(2,1)S(1)}, bf16[64,1,8,128]{3,0,2,1:T(8,128)(2,1)S(1)}, u32[]{:S(2)}, u32[]{:S(2)}) %collective-permute-start.9) | collective-permute-done | bytes 131104 | tf_op jit(solution)/shard_map/ppermute | solution.py:18
  146.0 7.7 %collective-permute-start.10 = (bf16[64,4,8,1]{3,0,2,1:T(8,128)(2,1)S(1)}, bf16[64,4,8,1]{3,0,2,1:T(8,128)(2,1)S(1)}, u32[]{:S(2)}, u32[]{:S(2)}) collective-permute-start(bf16[64,4,8,1]{3,0,2,1:T(8,128)(2,1)S(1)} %get-tuple-element.131), channel_id=1, source_target_pairs={{0,16},{16,32},{32,48},{48,64},{64,80},{80,96},{96,112},{1,17},{17... | collective-permute-start | bytes 12296 | tf_op jit(solution)/shard_map/ppermute | solution.py:17
  156.2 2.6 collective-permute-done.11
  187.1 3.8 collective-permute-start.12
  193.4 4.4 %collective-permute-done.13 = bf16[64,1,8,128]{3,0,2,1:T(8,128)(2,1)S(1)} collective-permute-done((bf16[64,1,8,128]{3,0,2,1:T(8,128)(2,1)S(1)}, bf16[64,1,8,128]{3,0,2,1:T(8,128)(2,1)S(1)}, u32[]{:S(2)}, u32[]{:S(2)}) %collective-permute-start.13) | collective-permute-done | bytes 131104 | tf_op jit(solution)/shard_map/ppermute | solution.py:18
  198.0 7.7 %collective-permute-start.14 = (bf16[64,4,8,1]{3,0,2,1:T(8,128)(2,1)S(1)}, bf16[64,4,8,1]{3,0,2,1:T(8,128)(2,1)S(1)}, u32[]{:S(2)}, u32[]{:S(2)}) collective-permute-start(bf16[64,4,8,1]{3,0,2,1:T(8,128)(2,1)S(1)} %get-tuple-element.129), channel_id=1, source_target_pairs={{0,16},{16,32},{32,48},{48,64},{64,80},{80,96},{96,112},{1,17},{17... | collective-permute-start | bytes 12296 | tf_op jit(solution)/shard_map/ppermute | solution.py:17
  207.4 3.9 collective-permute-done.15
  237.6 14.9 %all-to-all-start.2 = ((bf16[128,2,512]{2,1,0:T(2,128)(2,1)}), bf16[128,2,512]{2,1,0:T(2,128)(2,1)S(1)}, u32[]{:S(2)}, u32[]{:S(2)}) async-start(bf16[128,2,512]{2,1,0:T(2,128)(2,1)} %reshape.687), calls=%async_computation.2 | async-start | bytes 524288 | tf_op jit(solution)/shard_map/all_to_all | solution.py:127
  252.7 83.2 %all-reduce.9.cloned.1.call-done = (f32[27,64,64]{2,1,0:T(8,128)}, f32[27,64,64]{2,1,0:T(8,128)}, f32[8,64,64]{2,1,0:T(8,128)}) async-done(((f32[27,64,64]{2,1,0:T(8,128)}, f32[27,64,64]{2,1,0:T(8,128)}, f32[8,64,64]{2,1,0:T(8,128)}), (f32[27,64,64]{2,1,0:T(8,128)}, f32[27,64,64]{2,1,0:T(8,128)}, f32[8,64,64]{2,1,0:T(8,128)})) %all-reduce.9.cloned.1.call-update) | async-done | bytes 1015824 | tf_op jit(solution)/shard_map/psum | solution.py:129
  338.4 65.0 %all-reduce.11.cloned.1.call-done = (f32[27,64,64]{2,1,0:T(8,128)}, f32[27,64,64]{2,1,0:T(8,128)}, f32[8,64,64]{2,1,0:T(8,128)}) async-done(((f32[27,64,64]{2,1,0:T(8,128)}, f32[27,64,64]{2,1,0:T(8,128)}, f32[8,64,64]{2,1,0:T(8,128)}), (f32[27,64,64]{2,1,0:T(8,128)}, f32[27,64,64]{2,1,0:T(8,128)}, f32[8,64,64]{2,1,0:T(8,128)})) %all-reduce.11.cloned.1.call-update) | async-done | bytes 1015824 | tf_op jit(solution)/shard_map/psum | solution.py:129
  405.1 2.9 broadcast_multiply_fusion
  (374 shorter events, 132.5 us)
Async XLA Ops:
  7.2 39.7 %copy-start = (bf16[8,64,64]{2,1,0:T(8,128)(2,1)S(1)}, bf16[8,64,64]{2,1,0:T(8,128)(2,1)}, u32[]{:S(2)}) copy-start(bf16[8,64,64]{2,1,0:T(8,128)(2,1)} %param.11) | copy-start | bytes 196612
  9.8 20.6 %all-to-all-start.1 = ((s32[1,128,16]{2,0,1:T(1,128)}), s32[1,128,16]{2,0,1:T(1,128)S(1)}, u32[]{:S(2)}, u32[]{:S(2)}) async-start(s32[1,128,16]{2,0,1:T(1,128)} %bitcast.3), calls=%async_computation.1 | async-start | bytes 131072 | tf_op jit(solution)/shard_map/all_to_all | solution.py:86
  22.9 12.1 %copy-start.6 = (s32[2,8,128]{2,1,0:T(8,128)S(1)}, s32[2,8,128]{2,1,0:T(8,128)}, u32[]{:S(2)}) copy-start(s32[2,8,128]{2,1,0:T(8,128)} %param.14) | copy-start | bytes 24580
  30.4 15.5 %all-to-all-start = ((bf16[128,2,512]{2,1,0:T(2,128)(2,1)}), bf16[128,2,512]{2,1,0:T(2,128)(2,1)S(1)}, u32[]{:S(2)}, u32[]{:S(2)}) async-start(bf16[128,2,512]{2,1,0:T(2,128)(2,1)} %reshape.685), calls=%async_computation | async-start | bytes 524288 | tf_op jit(solution)/shard_map/all_to_all | solution.py:85
  35.0 300.9 %all-reduce.9.cloned.1.call-start = ((), (), s32[]{:S(2)}) async-start(), calls=%async_computation.3 | async-start | bytes 4063232 | tf_op jit(solution)/shard_map/psum | solution.py:129
  48.6 5.4 %collective-permute-start = (bf16[64,1,8,128]{3,0,2,1:T(8,128)(2,1)S(1)}, bf16[64,1,8,128]{3,0,2,1:T(8,128)(2,1)S(1)}, u32[]{:S(2)}, u32[]{:S(2)}) collective-permute-start(bf16[64,1,8,128]{3,0,2,1:T(8,128)(2,1)S(1)} %get-tuple-element.151), channel_id=1, source_target_pairs={{0,1},{1,2},{2,3},{3,4},{4,5},{5,6},{6,7},{7,8},{8,9},{9,10},{10,1... | collective-permute-start | bytes 393224 | tf_op jit(solution)/shard_map/ppermute | solution.py:17
  51.4 6.9 %collective-permute-start.1 = (bf16[64,1,8,128]{3,0,2,1:T(8,128)(2,1)S(1)}, bf16[64,1,8,128]{3,0,2,1:T(8,128)(2,1)S(1)}, u32[]{:S(2)}, u32[]{:S(2)}) collective-permute-start(bf16[64,1,8,128]{3,0,2,1:T(8,128)(2,1)S(1)} %get-tuple-element.152), channel_id=1, source_target_pairs={{1,0},{2,1},{3,2},{4,3},{5,4},{6,5},{7,6},{8,7},{9,8},{10,9},{11,1... | collective-permute-start | bytes 393224 | tf_op jit(solution)/shard_map/ppermute | solution.py:18
  58.6 4.3 %collective-permute-start.2 = (bf16[64,4,8,1]{3,0,2,1:T(8,128)(2,1)S(1)}, bf16[64,4,8,1]{3,0,2,1:T(8,128)(2,1)S(1)}, u32[]{:S(2)}, u32[]{:S(2)}) collective-permute-start(bf16[64,4,8,1]{3,0,2,1:T(8,128)(2,1)S(1)} %get-tuple-element.135), channel_id=1, source_target_pairs={{0,16},{16,32},{32,48},{48,64},{64,80},{80,96},{96,112},{1,17},{17... | collective-permute-start | bytes 12296 | tf_op jit(solution)/shard_map/ppermute | solution.py:17
  59.9 4.6 %collective-permute-start.3 = (bf16[64,4,8,1]{3,0,2,1:T(8,128)(2,1)S(1)}, bf16[64,4,8,1]{3,0,2,1:T(8,128)(2,1)S(1)}, u32[]{:S(2)}, u32[]{:S(2)}) collective-permute-start(bf16[64,4,8,1]{3,0,2,1:T(8,128)(2,1)S(1)} %get-tuple-element.136), channel_id=1, source_target_pairs={{16,0},{32,16},{48,32},{64,48},{80,64},{96,80},{112,96},{17,1},{33... | collective-permute-start | bytes 12296 | tf_op jit(solution)/shard_map/ppermute | solution.py:18
  83.8 4.8 %collective-permute-start.4 = (bf16[64,1,8,128]{3,0,2,1:T(8,128)(2,1)S(1)}, bf16[64,1,8,128]{3,0,2,1:T(8,128)(2,1)S(1)}, u32[]{:S(2)}, u32[]{:S(2)}) collective-permute-start(bf16[64,1,8,128]{3,0,2,1:T(8,128)(2,1)S(1)} %get-tuple-element.149), channel_id=1, source_target_pairs={{0,1},{1,2},{2,3},{3,4},{4,5},{5,6},{6,7},{7,8},{8,9},{9,10},{10,1... | collective-permute-start | bytes 393224 | tf_op jit(solution)/shard_map/ppermute | solution.py:17
  86.0 6.9 %collective-permute-start.5 = (bf16[64,1,8,128]{3,0,2,1:T(8,128)(2,1)S(1)}, bf16[64,1,8,128]{3,0,2,1:T(8,128)(2,1)S(1)}, u32[]{:S(2)}, u32[]{:S(2)}) collective-permute-start(bf16[64,1,8,128]{3,0,2,1:T(8,128)(2,1)S(1)} %get-tuple-element.150), channel_id=1, source_target_pairs={{1,0},{2,1},{3,2},{4,3},{5,4},{6,5},{7,6},{8,7},{9,8},{10,9},{11,1... | collective-permute-start | bytes 393224 | tf_op jit(solution)/shard_map/ppermute | solution.py:18
  93.2 9.6 %collective-permute-start.6 = (bf16[64,4,8,1]{3,0,2,1:T(8,128)(2,1)S(1)}, bf16[64,4,8,1]{3,0,2,1:T(8,128)(2,1)S(1)}, u32[]{:S(2)}, u32[]{:S(2)}) collective-permute-start(bf16[64,4,8,1]{3,0,2,1:T(8,128)(2,1)S(1)} %get-tuple-element.133), channel_id=1, source_target_pairs={{0,16},{16,32},{32,48},{48,64},{64,80},{80,96},{96,112},{1,17},{17... | collective-permute-start | bytes 12296 | tf_op jit(solution)/shard_map/ppermute | solution.py:17
  100.9 5.5 %collective-permute-start.7 = (bf16[64,4,8,1]{3,0,2,1:T(8,128)(2,1)S(1)}, bf16[64,4,8,1]{3,0,2,1:T(8,128)(2,1)S(1)}, u32[]{:S(2)}, u32[]{:S(2)}) collective-permute-start(bf16[64,4,8,1]{3,0,2,1:T(8,128)(2,1)S(1)} %get-tuple-element.134), channel_id=1, source_target_pairs={{16,0},{32,16},{48,32},{64,48},{80,64},{96,80},{112,96},{17,1},{33... | collective-permute-start | bytes 12296 | tf_op jit(solution)/shard_map/ppermute | solution.py:18
  133.3 8.0 %collective-permute-start.8 = (bf16[64,1,8,128]{3,0,2,1:T(8,128)(2,1)S(1)}, bf16[64,1,8,128]{3,0,2,1:T(8,128)(2,1)S(1)}, u32[]{:S(2)}, u32[]{:S(2)}) collective-permute-start(bf16[64,1,8,128]{3,0,2,1:T(8,128)(2,1)S(1)} %get-tuple-element.147), channel_id=1, source_target_pairs={{0,1},{1,2},{2,3},{3,4},{4,5},{5,6},{6,7},{7,8},{8,9},{9,10},{10,1... | collective-permute-start | bytes 393224 | tf_op jit(solution)/shard_map/ppermute | solution.py:17
  138.8 6.9 %collective-permute-start.9 = (bf16[64,1,8,128]{3,0,2,1:T(8,128)(2,1)S(1)}, bf16[64,1,8,128]{3,0,2,1:T(8,128)(2,1)S(1)}, u32[]{:S(2)}, u32[]{:S(2)}) collective-permute-start(bf16[64,1,8,128]{3,0,2,1:T(8,128)(2,1)S(1)} %get-tuple-element.148), channel_id=1, source_target_pairs={{1,0},{2,1},{3,2},{4,3},{5,4},{6,5},{7,6},{8,7},{9,8},{10,9},{11,1... | collective-permute-start | bytes 393224 | tf_op jit(solution)/shard_map/ppermute | solution.py:18
  146.0 9.5 %collective-permute-start.10 = (bf16[64,4,8,1]{3,0,2,1:T(8,128)(2,1)S(1)}, bf16[64,4,8,1]{3,0,2,1:T(8,128)(2,1)S(1)}, u32[]{:S(2)}, u32[]{:S(2)}) collective-permute-start(bf16[64,4,8,1]{3,0,2,1:T(8,128)(2,1)S(1)} %get-tuple-element.131), channel_id=1, source_target_pairs={{0,16},{16,32},{32,48},{48,64},{64,80},{80,96},{96,112},{1,17},{17... | collective-permute-start | bytes 12296 | tf_op jit(solution)/shard_map/ppermute | solution.py:17
  153.7 5.2 %collective-permute-start.11 = (bf16[64,4,8,1]{3,0,2,1:T(8,128)(2,1)S(1)}, bf16[64,4,8,1]{3,0,2,1:T(8,128)(2,1)S(1)}, u32[]{:S(2)}, u32[]{:S(2)}) collective-permute-start(bf16[64,4,8,1]{3,0,2,1:T(8,128)(2,1)S(1)} %get-tuple-element.132), channel_id=1, source_target_pairs={{16,0},{32,16},{48,32},{64,48},{80,64},{96,80},{112,96},{17,1},{33... | collective-permute-start | bytes 12296 | tf_op jit(solution)/shard_map/ppermute | solution.py:18
  187.1 6.3 %collective-permute-start.12 = (bf16[64,1,8,128]{3,0,2,1:T(8,128)(2,1)S(1)}, bf16[64,1,8,128]{3,0,2,1:T(8,128)(2,1)S(1)}, u32[]{:S(2)}, u32[]{:S(2)}) collective-permute-start(bf16[64,1,8,128]{3,0,2,1:T(8,128)(2,1)S(1)} %get-tuple-element.145), channel_id=1, source_target_pairs={{0,1},{1,2},{2,3},{3,4},{4,5},{5,6},{6,7},{7,8},{8,9},{9,10},{10,1... | collective-permute-start | bytes 393224 | tf_op jit(solution)/shard_map/ppermute | solution.py:17
  190.9 6.9 %collective-permute-start.13 = (bf16[64,1,8,128]{3,0,2,1:T(8,128)(2,1)S(1)}, bf16[64,1,8,128]{3,0,2,1:T(8,128)(2,1)S(1)}, u32[]{:S(2)}, u32[]{:S(2)}) collective-permute-start(bf16[64,1,8,128]{3,0,2,1:T(8,128)(2,1)S(1)} %get-tuple-element.146), channel_id=1, source_target_pairs={{1,0},{2,1},{3,2},{4,3},{5,4},{6,5},{7,6},{8,7},{9,8},{10,9},{11,1... | collective-permute-start | bytes 393224 | tf_op jit(solution)/shard_map/ppermute | solution.py:18
  198.0 9.3 %collective-permute-start.14 = (bf16[64,4,8,1]{3,0,2,1:T(8,128)(2,1)S(1)}, bf16[64,4,8,1]{3,0,2,1:T(8,128)(2,1)S(1)}, u32[]{:S(2)}, u32[]{:S(2)}) collective-permute-start(bf16[64,4,8,1]{3,0,2,1:T(8,128)(2,1)S(1)} %get-tuple-element.129), channel_id=1, source_target_pairs={{0,16},{16,32},{32,48},{48,64},{64,80},{80,96},{96,112},{1,17},{17... | collective-permute-start | bytes 12296 | tf_op jit(solution)/shard_map/ppermute | solution.py:17
  205.8 5.5 %collective-permute-start.15 = (bf16[64,4,8,1]{3,0,2,1:T(8,128)(2,1)S(1)}, bf16[64,4,8,1]{3,0,2,1:T(8,128)(2,1)S(1)}, u32[]{:S(2)}, u32[]{:S(2)}) collective-permute-start(bf16[64,4,8,1]{3,0,2,1:T(8,128)(2,1)S(1)} %get-tuple-element.130), channel_id=1, source_target_pairs={{16,0},{32,16},{48,32},{64,48},{80,64},{96,80},{112,96},{17,1},{33... | collective-permute-start | bytes 12296 | tf_op jit(solution)/shard_map/ppermute | solution.py:18
  236.3 16.2 %copy-start.7 = (s32[1,128]{1,0:T(1,128)S(1)}, s32[1,128]{1,0:T(1,128)}, u32[]{:S(2)}) copy-start(s32[1,128]{1,0:T(1,128)} %param.10) | copy-start | bytes 1540
  237.6 99.2 %all-to-all-start.2 = ((bf16[128,2,512]{2,1,0:T(2,128)(2,1)}), bf16[128,2,512]{2,1,0:T(2,128)(2,1)S(1)}, u32[]{:S(2)}, u32[]{:S(2)}) async-start(bf16[128,2,512]{2,1,0:T(2,128)(2,1)} %reshape.687), calls=%async_computation.2 | async-start | bytes 524288 | tf_op jit(solution)/shard_map/all_to_all | solution.py:127
  252.5 150.9 %all-reduce.11.cloned.1.call-start = ((), (), s32[]{:S(2)}) async-start(), calls=%async_computation.4 | async-start | bytes 4063232 | tf_op jit(solution)/shard_map/psum | solution.py:129
  (5 other events, 7.8 us)
Sparse Core Ops, SparseCore 0:
  235.8 100.0 all-reduce.8
  338.4 64.8 all-reduce.10
